TPU v7x, 32 devices: a whole 2x2x4 slice. The times are simulated.
32 devices in a mesh: own: 8 (over z, y), rep: 4 (over x, core).
Axes of the slice: x: 2, y: 2, z: 4, core: 2. Of those that a mesh axis runs over, the one named last changes fastest.
Arguments:
- hidden: bfloat16 [1024, 1024], P('own', 'rep'), may hold values from -140 to 140
- weight: bfloat16 [8, 2048, 1024], P('own', None, 'rep'), may hold values from -0.1875 to 0.1875
- bucket_map: int32 [8], replicated, may hold values from 0 to 7, each once
- active: int32 [1024, 2], P('own'), may hold values from 0 to 7, all different within a row; in each aligned block of 128 rows (0 to 127, 128 to 255, ...) at most 64 rows name the same one
- label_pick: int32 [1024], P('own'), may hold values from 0 to 4095
Outputs:
- sample_loss: float32 [1024], P('own')
- grad_hidden: float32 [1024, 1024], P('own', 'rep')
- grad_weight: bfloat16 [8, 2048, 1024], P('own', None, 'rep')
Inputs may be any that keep to these rules, and one draw needn't show every extreme that they name: `bucket_map`: each weight slot is named once. `active`: A sample's 2 bucket ids differ. Among the 128 samples of one index of own, no bucket is named by more than 64 samples, a bound that some block reaches.
All inputs are finite; a program needn't handle non-finite values.
Results may differ from a plain program's by a relative error of at most 0.0032.
Values may be sent and summed in bfloat16 or wider, within the bound.
A program may use at most 64 MiB of HBM per device.

v0:
```python
import jax
import jax.numpy as jnp
from jax import lax
from jax.sharding import PartitionSpec as P


def body(hidden, weight, bucket_map, active, label_pick):
    samp_count = hidden.shape[0]
    bucket_dev, label_count, feature_part = weight.shape
    picks = active.shape[1]
    bucket_total = bucket_map.shape[0]
    owner_count = lax.axis_size("own")
    slot_depth = max(2, 2 * samp_count * picks // bucket_total)
    pair_count = samp_count * picks
    slots_total = bucket_total * slot_depth
    row_count = owner_count * slot_depth
    pair_bucket = active.reshape(pair_count)
    bucket_iota = lax.broadcasted_iota(jnp.int32, (pair_count, bucket_total), 1)
    slot_index = jnp.sum(
        jnp.where(pair_bucket[:, None] == bucket_iota, bucket_map[None, :], 0), axis=1
    )
    slot_hits = (slot_index[:, None] == bucket_iota).astype(jnp.int32)
    earlier = jnp.cumsum(slot_hits, axis=0) - slot_hits
    rank_within = jnp.sum(earlier * slot_hits, axis=1)
    position = slot_index * slot_depth + rank_within
    pair_index = jnp.arange(pair_count, dtype=jnp.int32)
    pick_value = jnp.repeat(label_pick, picks)
    target_pair = jnp.where(
        pick_value // label_count == pair_index % picks, pick_value % label_count, -1
    )
    width_sent = hidden.shape[1]
    pair_rows = jnp.repeat(hidden, picks, axis=0)
    send_rows = jnp.zeros((slots_total, width_sent), jnp.bfloat16).at[position].set(pair_rows)
    send_target = jnp.full((slots_total,), -1, jnp.int32).at[position].set(target_pair)
    got_rows, got_target = (
        lax.all_to_all(
            send_rows.reshape(owner_count, bucket_dev * slot_depth, width_sent),
            "own",
            split_axis=0,
            concat_axis=0,
            tiled=True,
        ),
        lax.all_to_all(
            send_target.reshape(owner_count, bucket_dev * slot_depth),
            "own",
            split_axis=0,
            concat_axis=0,
            tiled=True,
        ),
    )
    received = got_rows.reshape(owner_count, bucket_dev, slot_depth, width_sent).transpose(
        1, 0, 2, 3
    )
    received = received.reshape(bucket_dev, row_count, width_sent)
    target_col = (
        got_target.reshape(owner_count, bucket_dev, slot_depth)
        .transpose(1, 0, 2)
        .reshape(bucket_dev, row_count)
    )
    partial_value = jnp.einsum("brd,bcd->brc", received, weight, preferred_element_type=jnp.float32)
    logits = lax.psum(partial_value, "rep")
    columns = lax.broadcasted_iota(jnp.int32, (1, 1, label_count), 2)
    row_max = jnp.max(logits, axis=2)
    row_sum = jnp.sum(jnp.exp(logits - row_max[..., None]), axis=2)
    row_target = jnp.sum(jnp.where(columns == target_col[..., None], logits, 0.0), axis=2)

    def to_sources(values):
        return (
            values.reshape(bucket_dev, owner_count, slot_depth)
            .transpose(1, 0, 2)
            .reshape(owner_count, bucket_dev * slot_depth)
        )

    back_max, back_sum, back_target = (
        lax.all_to_all(to_sources(row_max), "own", split_axis=0, concat_axis=0, tiled=True),
        lax.all_to_all(to_sources(row_sum), "own", split_axis=0, concat_axis=0, tiled=True),
        lax.all_to_all(to_sources(row_target), "own", split_axis=0, concat_axis=0, tiled=True),
    )
    pair_max = back_max.reshape(slots_total)[position].reshape(samp_count, picks)
    pair_sum = back_sum.reshape(slots_total)[position].reshape(samp_count, picks)
    pair_target = back_target.reshape(slots_total)[position].reshape(samp_count, picks)
    peak_max = jnp.max(pair_max, axis=1)
    norm_sum = jnp.sum(pair_sum * jnp.exp(pair_max - peak_max[:, None]), axis=1)
    log_norm = peak_max + jnp.log(norm_sum)
    sample_loss = log_norm - jnp.sum(pair_target, axis=1)
    send_norm = jnp.zeros((slots_total,), jnp.float32).at[position].set(jnp.repeat(log_norm, picks))
    got_norm = lax.all_to_all(
        send_norm.reshape(owner_count, bucket_dev * slot_depth),
        "own",
        split_axis=0,
        concat_axis=0,
        tiled=True,
    )
    row_norm = (
        got_norm.reshape(owner_count, bucket_dev, slot_depth)
        .transpose(1, 0, 2)
        .reshape(bucket_dev, row_count)
    )
    onehot = (columns == target_col[..., None]).astype(jnp.float32)
    grad_logits = (jnp.exp(logits - row_norm[..., None]) - onehot).astype(jnp.bfloat16)
    grad_weight = jnp.einsum(
        "brc,brd->bcd", grad_logits, received, preferred_element_type=jnp.float32
    ).astype(jnp.bfloat16)
    row_grads = jnp.einsum("brc,bcd->brd", grad_logits, weight, preferred_element_type=jnp.float32)
    send_grads = row_grads.reshape(bucket_dev, owner_count, slot_depth, feature_part).transpose(
        1, 0, 2, 3
    )
    send_grads = send_grads.reshape(owner_count, bucket_dev * slot_depth, feature_part)
    got_grads = lax.all_to_all(send_grads, "own", split_axis=0, concat_axis=0, tiled=True)
    pair_grads = got_grads.reshape(slots_total, feature_part)[position].reshape(
        samp_count, picks, feature_part
    )
    grad_hidden = jnp.sum(pair_grads, axis=1)
    return (sample_loss, grad_hidden, grad_weight)


def solution(mesh):
    in_specs = (P("own", "rep"), P("own", None, "rep"), P(), P("own", None), P("own"))
    out_specs = (P("own"), P("own", "rep"), P("own", None, "rep"))
    return jax.shard_map(body, mesh=mesh, in_specs=in_specs, out_specs=out_specs, check_vma=False)
```

profile of v0, /device:TPU:0, one launch (start us, length us, event | category | flops | bytes accessed | tf_op | source)
XLA Modules:
  0.0 201.0 jit_solution(17374603025491268575)
XLA Ops:
  7.2 0.0 all-reduce.2.cloned.1.call-start
  7.2 0.9 copy.8
  8.1 0.1 eq.66
  8.2 0.7 select_reduce_fusion.1
  9.0 0.6 reduce-window.6
  9.6 0.2 slice_reduce_fusion
  9.8 0.1 fusion.8
  9.9 0.9 broadcast_in_dim.50
  10.8 0.1 reshape.272
  10.9 1.5 scatter_custom_fusion
  12.5 16.0 %all_to_all.55 = bf16[8,64,256]{2,1,0:T(8,128)(2,1)S(1)} all-to-all(bf16[8,64,256]{2,1,0:T(8,128)(2,1)S(1)} %bitcast.33), channel_id=1, replica_groups=mesh['own'=8,'rep'=4] {'own'}, dimensions={0} | all-to-all | bytes 524288 | tf_op jit(solution)/shard_map/all_to_all | solution.py:36
  28.5 2.7 %convolution_bitcast_fusion = f32[1,512,2048]{2,1,0:T(8,128)} fusion(bf16[512,256]{1,0:T(8,128)(2,1)S(1)} %bitcast.34, bf16[1,2048,256]{2,1,0:T(8,128)(2,1)S(1)} %copy-done), kind=kOutput, calls=%fused_computation.11 | convolution fusion | flops 536870912 | bytes 5505024 | tf_op jit(solution)/shard_map/brd,bcd->brc/dot_general | solution.py:60
  31.2 0.1 broadcast_in_dim.52
  31.3 0.1 reshape.229
  31.5 1.4 scatter_custom_fusion.1
  32.9 0.1 all_to_all.41
  32.9 9.8 %all_to_all.56 = s32[8,1,64]{2,1,0:T(1,128)S(1)} all-to-all(s32[8,1,64]{2,1,0:T(1,128)S(1)} %all_to_all.41), channel_id=1, replica_groups=mesh['own'=8,'rep'=4] {'own'}, dimensions={0} | all-to-all | bytes 4096 | tf_op jit(solution)/shard_map/all_to_all | solution.py:43
  42.8 0.5 broadcast.131
  43.3 0.7 reduce.22
  44.0 0.1 eq.76
  44.0 71.8 %all-reduce.2.cloned.1.call-done = f32[1,512,2048]{2,1,0:T(8,128)} async-done(((f32[1,512,2048]{2,1,0:T(8,128)}), f32[1,512,2048]{2,1,0:T(8,128)}) %all-reduce.2.cloned.1.call-update) | async-done | bytes 4194320 | tf_op jit(solution)/shard_map/psum | solution.py:61
  115.8 2.5 %reduce_max.18 = f32[512]{0:T(512)S(1)} reduce(f32[1,512,2048]{2,1,0:T(8,128)} %all-reduce.2.cloned.1.call-done, f32[]{:T(128)} %constant.50.clone.1), dimensions={0,2}, to_apply=%region_6.7 | reduce | flops 1048064 | bytes 4196356 | tf_op jit(solution)/shard_map/reduce_max | solution.py:63
  118.3 3.6 %select_reduce_fusion = (f32[512]{0:T(512)S(1)}, f32[512]{0:T(512)S(1)}) fusion(f32[1,512,2048]{2,1,0:T(8,128)} %all-reduce.2.cloned.1.call-done, s32[512]{0:T(512)S(1)} %eq.76, f32[512]{0:T(512)S(1)} %reduce_max.18), kind=kLoop, calls=%fused_computation.8 | loop fusion | flops 5241856 | bytes 4202496 | tf_op jit(solution)/shard_map/reduce_sum | solution.py:65
  121.9 0.7 all_to_all.39
  122.6 5.5 %all-to-all-start.2 = ((f32[8,1,64]{2,1,0:T(1,128)}), f32[8,1,64]{2,1,0:T(1,128)S(1)}, u32[]{:S(2)}, u32[]{:S(2)}) async-start(f32[8,1,64]{2,1,0:T(1,128)} %all_to_all.39), calls=%async_computation.2 | async-start | bytes 8192 | tf_op jit(solution)/shard_map/all_to_all | solution.py:76
  128.1 0.7 all_to_all.37
  128.8 5.7 %all-to-all-done.2 = f32[8,1,64]{2,1,0:T(1,128)S(1)} async-done(((f32[8,1,64]{2,1,0:T(1,128)}), f32[8,1,64]{2,1,0:T(1,128)S(1)}, u32[]{:S(2)}, u32[]{:S(2)}) %all-to-all-start.2) | async-done | bytes 2080 | tf_op jit(solution)/shard_map/all_to_all | solution.py:76
  134.5 3.3 %all-to-all-start.1 = ((f32[8,1,64]{2,1,0:T(1,128)}), f32[8,1,64]{2,1,0:T(1,128)S(1)}, u32[]{:S(2)}, u32[]{:S(2)}) async-start(f32[8,1,64]{2,1,0:T(1,128)} %all_to_all.37), calls=%async_computation.1 | async-start | bytes 8192 | tf_op jit(solution)/shard_map/all_to_all | solution.py:75
  137.8 0.7 all_to_all.43
  138.5 5.7 %all-to-all-done.1 = f32[8,1,64]{2,1,0:T(1,128)S(1)} async-done(((f32[8,1,64]{2,1,0:T(1,128)}), f32[8,1,64]{2,1,0:T(1,128)S(1)}, u32[]{:S(2)}, u32[]{:S(2)}) %all-to-all-start.1) | async-done | bytes 2080 | tf_op jit(solution)/shard_map/all_to_all | solution.py:75
  144.2 3.3 %all-to-all-start.4 = ((f32[8,1,64]{2,1,0:T(1,128)}), f32[8,1,64]{2,1,0:T(1,128)S(1)}, u32[]{:S(2)}, u32[]{:S(2)}) async-start(f32[8,1,64]{2,1,0:T(1,128)} %all_to_all.43), calls=%async_computation.4 | async-start | bytes 8192 | tf_op jit(solution)/shard_map/all_to_all | solution.py:77
  147.5 0.5 broadcast.129
  148.0 0.7 reduce.21
  148.7 0.1 reshape.227
  148.7 1.9 gather_fusion.1
  150.7 0.1 reshape.228
  150.8 0.7 reduce.20
  151.5 0.1 reshape.225
  151.6 1.9 gather_fusion
  153.5 0.1 reshape.226
  153.7 0.1 reduce_max.19
  153.8 0.7 reduce.23
  154.5 0.1 reshape.230
  154.5 1.9 gather_fusion.2
  156.5 0.1 reshape.231
  156.6 0.2 multiply_reduce_fusion
  156.8 0.1 reduce_sum.68
  156.9 0.5 fusion.14
  157.5 0.1 broadcast_in_dim.55
  157.5 0.1 reshape.288
  157.7 1.4 scatter_custom_fusion.2
  159.1 0.1 all_to_all.45
  159.2 12.2 %all_to_all.57 = f32[8,1,64]{2,1,0:T(1,128)S(1)} all-to-all(f32[8,1,64]{2,1,0:T(1,128)S(1)} %all_to_all.45), channel_id=1, replica_groups=mesh['own'=8,'rep'=4] {'own'}, dimensions={0} | all-to-all | bytes 4096 | tf_op jit(solution)/shard_map/all_to_all | solution.py:87
  171.4 0.7 reduce.24
  172.0 0.1 sub.48
  172.1 3.3 %subtract_convert_fusion = bf16[1,512,2048]{2,1,0:T(8,128)(2,1)S(1)} fusion(f32[1,512,2048]{2,1,0:T(8,128)} %all-reduce.2.cloned.1.call-done, f32[512]{0:T(512)S(1)} %sub.48, s32[512]{0:T(512)S(1)} %eq.76), kind=kLoop, calls=%fused_computation.7 | loop fusion | flops 5242880 | bytes 6295552 | tf_op jit(solution)/shard_map/convert_element_type | solution.py:100
  175.4 1.3 copy-done.1
  176.8 1.5 fusion.2
  178.3 3.5 %all-to-all-start.6 = ((f32[8,64,256]{2,1,0:T(8,128)}), f32[8,64,256]{2,1,0:T(8,128)S(1)}, u32[]{:S(2)}, u32[]{:S(2)}) async-start(f32[8,64,256]{2,1,0:T(8,128)} %fusion.2), calls=%async_computation.6 | async-start | bytes 1048576 | tf_op jit(solution)/shard_map/all_to_all | solution.py:109
  181.8 3.3 %fusion = bf16[1,2048,256]{2,1,0:T(8,128)(2,1)} fusion(bf16[512,256]{1,0:T(8,128)(2,1)S(1)} %bitcast.35, bf16[1,512,2048]{2,1,0:T(8,128)(2,1)} %copy-done.1), kind=kOutput, calls=%fused_computation.13 | convolution fusion | flops 537395200 | bytes 3407872 | tf_op jit(solution)/shard_map/brc,brd->bcd/dot_general | solution.py:101
  185.1 6.9 %all-to-all-done.6 = f32[8,64,256]{2,1,0:T(8,128)S(1)} async-done(((f32[8,64,256]{2,1,0:T(8,128)}), f32[8,64,256]{2,1,0:T(8,128)S(1)}, u32[]{:S(2)}, u32[]{:S(2)}) %all-to-all-start.6) | async-done | bytes 524320 | tf_op jit(solution)/shard_map/all_to_all | solution.py:109
  192.0 1.0 gather_fusion.3
  193.0 0.1 reshape.234
  193.2 1.0 reduce_sum.69
  (14 shorter events, 0.1 us)
Async XLA Ops:
  7.2 21.3 %copy-start = (bf16[1,2048,256]{2,1,0:T(8,128)(2,1)S(1)}, bf16[1,2048,256]{2,1,0:T(8,128)(2,1)}, u32[]{:S(2)}) copy-start(bf16[1,2048,256]{2,1,0:T(8,128)(2,1)} %param.6) | copy-start | bytes 3145732
  7.2 108.6 %all-reduce.2.cloned.1.call-start = ((), (), s32[]{:S(2)}) async-start(), calls=%async_computation.7 | async-start | bytes 8388608 | tf_op jit(solution)/shard_map/psum | solution.py:61
  28.5 2.7 %copy-start.2 = (s32[128]{0:T(128)S(1)}, s32[128]{0:T(128)}, u32[]{:S(2)}) copy-start(s32[128]{0:T(128)} %param.9) | copy-start | bytes 1540
  122.6 11.9 %all-to-all-start.2 = ((f32[8,1,64]{2,1,0:T(1,128)}), f32[8,1,64]{2,1,0:T(1,128)S(1)}, u32[]{:S(2)}, u32[]{:S(2)}) async-start(f32[8,1,64]{2,1,0:T(1,128)} %all_to_all.39), calls=%async_computation.2 | async-start | bytes 8192 | tf_op jit(solution)/shard_map/all_to_all | solution.py:76
  134.5 9.6 %all-to-all-start.1 = ((f32[8,1,64]{2,1,0:T(1,128)}), f32[8,1,64]{2,1,0:T(1,128)S(1)}, u32[]{:S(2)}, u32[]{:S(2)}) async-start(f32[8,1,64]{2,1,0:T(1,128)} %all_to_all.37), calls=%async_computation.1 | async-start | bytes 8192 | tf_op jit(solution)/shard_map/all_to_all | solution.py:75
  144.2 9.6 %all-to-all-start.4 = ((f32[8,1,64]{2,1,0:T(1,128)}), f32[8,1,64]{2,1,0:T(1,128)S(1)}, u32[]{:S(2)}, u32[]{:S(2)}) async-start(f32[8,1,64]{2,1,0:T(1,128)} %all_to_all.43), calls=%async_computation.4 | async-start | bytes 8192 | tf_op jit(solution)/shard_map/all_to_all | solution.py:77
  175.4 1.4 copy-start.1
  178.3 13.7 %all-to-all-start.6 = ((f32[8,64,256]{2,1,0:T(8,128)}), f32[8,64,256]{2,1,0:T(8,128)S(1)}, u32[]{:S(2)}, u32[]{:S(2)}) async-start(f32[8,64,256]{2,1,0:T(8,128)} %fusion.2), calls=%async_computation.6 | async-start | bytes 1048576 | tf_op jit(solution)/shard_map/all_to_all | solution.py:109
Sparse Core Ops, SparseCore 0:
  31.3 84.4 all-reduce.1
where the time goes:
time: 202 us; the launch traced here: 201 us
  waiting for transfers between devices  90.1 us (45%)
  blocking collectives  38 us (19%)
  local copies, waits for them, and re-layouts  19.3 us (10%)
  other arithmetic  16.1 us (8%)
  starting transfers between devices  15.7 us (8%)
  between operations  14.3 us (7%)
  matrix products  7.55 us (4%)
    psum x1, waiting for transfers between devices, body(): logits = lax.psum(partial_value, 'rep')  71.8 us
    all_to_all x1, blocking collectives, body(): lax.all_to_all(send_rows.reshape(owner_count, bucket_dev * slot_depth, wi...  16 us
    all_to_all x1, blocking collectives, body(): lax.all_to_all(send_norm.reshape(owner_count, bucket_dev * slot_depth), '...  12.2 us
    all_to_all x1, blocking collectives, body(): lax.all_to_all(send_target.reshape(owner_count, bucket_dev * slot_depth),...  9.84 us
    all_to_all x1, waiting for transfers between devices, body(): lax.all_to_all(send_grads, 'own', split_axis=0, concat_axis=0, tiled=True)  6.92 us
    all_to_all x1, waiting for transfers between devices, body(): lax.all_to_all(to_sources(row_sum), 'own', split_axis=0, concat_axis=0, t...  5.72 us
    all_to_all x1, waiting for transfers between devices, body(): lax.all_to_all(to_sources(row_max), 'own', split_axis=0, concat_axis=0, t...  5.65 us
    all_to_all x1, starting transfers between devices, body(): lax.all_to_all(to_sources(row_sum), 'own', split_axis=0, concat_axis=0, t...  5.52 us
  transfers between devices with their start and end apart: 5, of which 4 were waited for; matrix products, arithmetic and copies ran while one was open for 6% of the time, Pallas kernels for 0%

commit v1 on v0

--- a/solution.py
+++ b/solution.py
@@ -58,7 +58,7 @@
         .reshape(bucket_dev, row_count)
     )
     partial_value = jnp.einsum("brd,bcd->brc", received, weight, preferred_element_type=jnp.float32)
-    logits = lax.psum(partial_value, "rep")
+    logits = jnp.sum(lax.all_gather(partial_value, "rep"), axis=0)
     columns = lax.broadcasted_iota(jnp.int32, (1, 1, label_count), 2)
     row_max = jnp.max(logits, axis=2)
     row_sum = jnp.sum(jnp.exp(logits - row_max[..., None]), axis=2)

time: 202 us -> 231 us (1.14)
  waiting for transfers between devices: 90.1 us -> 110 us
  other arithmetic: 16.1 us -> 26.2 us
    all_gather x0 -> x1, waiting for transfers between devices: none -> 92.2 us  [body(): logits = jnp.sum(lax.all_gather(partial_value, 'rep'), axis=0)]
    psum x1 -> x0, waiting for transfers between devices: 71.8 us -> none  [body(): logits = lax.psum(partial_value, 'rep')]
    reduce_sum x0 -> x1, other arithmetic: none -> 10.1 us  [body(): logits = jnp.sum(lax.all_gather(partial_value, 'rep'), axis=0)]
where the time goes in v1:
time: 231 us
  waiting for transfers between devices  110 us (48%)
  blocking collectives  38 us (16%)
  other arithmetic  26.2 us (11%)
  local copies, waits for them, and re-layouts  17.9 us (8%)
  starting transfers between devices  15.7 us (7%)
  between operations  14.3 us (6%)
  matrix products  8.91 us (4%)
    all_gather x1, waiting for transfers between devices, body(): logits = jnp.sum(lax.all_gather(partial_value, 'rep'), axis=0)  92.2 us
    all_to_all x1, blocking collectives, body(): lax.all_to_all(send_rows.reshape(owner_count, bucket_dev * slot_depth, wi...  16 us
    all_to_all x1, blocking collectives, body(): lax.all_to_all(send_norm.reshape(owner_count, bucket_dev * slot_depth), '...  12.2 us
    reduce_sum x1, other arithmetic, body(): logits = jnp.sum(lax.all_gather(partial_value, 'rep'), axis=0)  10.1 us
    all_to_all x1, blocking collectives, body(): lax.all_to_all(send_target.reshape(owner_count, bucket_dev * slot_depth),...  9.84 us
    all_to_all x1, waiting for transfers between devices, body(): lax.all_to_all(send_grads, 'own', split_axis=0, concat_axis=0, tiled=True)  6.07 us
    all_to_all x1, waiting for transfers between devices, body(): lax.all_to_all(to_sources(row_sum), 'own', split_axis=0, concat_axis=0, t...  5.72 us
    all_to_all x1, waiting for transfers between devices, body(): lax.all_to_all(to_sources(row_max), 'own', split_axis=0, concat_axis=0, t...  5.65 us
  transfers between devices with their start and end apart: 5, of which 4 were waited for; matrix products, arithmetic and copies ran while one was open for 6% of the time, Pallas kernels for 0%

profile of v1, /device:TPU:0, one launch (start us, length us, event | category | flops | bytes accessed | tf_op | source)
XLA Modules:
  0.0 230.7 jit_solution(2563021903725055692)
XLA Ops:
  7.2 0.0 all-gather.3.cloned.1.call-start
  7.2 0.9 copy.8
  8.1 0.1 eq.88
  8.2 0.7 select_reduce_fusion.1
  9.0 0.6 reduce-window.6
  9.6 0.2 slice_reduce_fusion
  9.8 0.1 fusion.15
  9.9 0.9 broadcast_in_dim.50
  10.8 0.1 reshape.425
  10.9 1.5 scatter_custom_fusion
  12.5 16.0 %all_to_all.55 = bf16[8,64,256]{2,1,0:T(8,128)(2,1)S(1)} all-to-all(bf16[8,64,256]{2,1,0:T(8,128)(2,1)S(1)} %bitcast.44), channel_id=1, replica_groups=mesh['own'=8,'rep'=4] {'own'}, dimensions={0} | all-to-all | bytes 524288 | tf_op jit(solution)/shard_map/all_to_all | solution.py:36
  28.5 2.7 %fusion.10 = f32[512,2048]{1,0:T(8,128)} fusion(bf16[512,256]{1,0:T(8,128)(2,1)S(1)} %bitcast.45, bf16[1,2048,256]{2,1,0:T(8,128)(2,1)S(1)} %copy-done), kind=kOutput, calls=%fused_computation.23 | convolution fusion | flops 536870912 | bytes 5505024 | tf_op jit(solution)/shard_map/brd,bcd->brc/dot_general | solution.py:60
  31.2 0.1 broadcast_in_dim.52
  31.2 0.1 reshape.383
  31.4 1.4 scatter_custom_fusion.1
  32.8 0.1 all_to_all.41
  32.9 9.8 %all_to_all.56 = s32[8,1,64]{2,1,0:T(1,128)S(1)} all-to-all(s32[8,1,64]{2,1,0:T(1,128)S(1)} %all_to_all.41), channel_id=1, replica_groups=mesh['own'=8,'rep'=4] {'own'}, dimensions={0} | all-to-all | bytes 4096 | tf_op jit(solution)/shard_map/all_to_all | solution.py:43
  42.7 0.5 broadcast.183
  43.2 0.7 reduce.28
  43.9 0.1 eq.98
  44.0 92.2 %all-gather.3.cloned.1.call-done = f32[2048,2048]{1,0:T(8,128)} async-done(((f32[512,2048]{1,0:T(8,128)}), f32[2048,2048]{1,0:T(8,128)}) %all-gather.3.cloned.1.call-update) | async-done | bytes 16777232 | tf_op jit(solution)/shard_map/all_gather | solution.py:61
  136.2 10.1 %reduce.7 = f32[512,2048]{1,0:T(8,128)} reduce(f32[4,512,2048]{2,1,0:T(8,128)} %bitcast.41, f32[]{:T(128)} %constant.50.clone.1), dimensions={0}, to_apply=%region_5.6 | reduce | flops 3145728 | bytes 20971524 | tf_op jit(solution)/shard_map/reduce_sum | solution.py:61
  146.3 2.5 %reduce_max.18 = f32[512]{0:T(512)S(1)} reduce(f32[512,2048]{1,0:T(8,128)} %reduce.7, f32[]{:T(128)} %constant.51.clone.1), dimensions={1}, to_apply=%region_6.7 | reduce | flops 1048064 | bytes 4196356 | tf_op jit(solution)/shard_map/reduce_max | solution.py:63
  148.8 3.6 %select_reduce_fusion = (f32[512]{0:T(512)S(1)}, f32[512]{0:T(512)S(1)}) fusion(f32[512,2048]{1,0:T(8,128)} %reduce.7, s32[512]{0:T(512)S(1)} %eq.98, f32[512]{0:T(512)S(1)} %reduce_max.18), kind=kLoop, calls=%fused_computation.13 | loop fusion | flops 5241856 | bytes 4202496 | tf_op jit(solution)/shard_map/reduce_sum | solution.py:65
  152.4 0.7 all_to_all.39
  153.1 5.5 %all-to-all-start.2 = ((f32[8,1,64]{2,1,0:T(1,128)}), f32[8,1,64]{2,1,0:T(1,128)S(1)}, u32[]{:S(2)}, u32[]{:S(2)}) async-start(f32[8,1,64]{2,1,0:T(1,128)} %all_to_all.39), calls=%async_computation.2 | async-start | bytes 8192 | tf_op jit(solution)/shard_map/all_to_all | solution.py:76
  158.6 0.7 all_to_all.37
  159.3 5.7 %all-to-all-done.2 = f32[8,1,64]{2,1,0:T(1,128)S(1)} async-done(((f32[8,1,64]{2,1,0:T(1,128)}), f32[8,1,64]{2,1,0:T(1,128)S(1)}, u32[]{:S(2)}, u32[]{:S(2)}) %all-to-all-start.2) | async-done | bytes 2080 | tf_op jit(solution)/shard_map/all_to_all | solution.py:76
  165.0 3.3 %all-to-all-start.1 = ((f32[8,1,64]{2,1,0:T(1,128)}), f32[8,1,64]{2,1,0:T(1,128)S(1)}, u32[]{:S(2)}, u32[]{:S(2)}) async-start(f32[8,1,64]{2,1,0:T(1,128)} %all_to_all.37), calls=%async_computation.1 | async-start | bytes 8192 | tf_op jit(solution)/shard_map/all_to_all | solution.py:75
  168.3 0.7 all_to_all.43
  169.0 5.7 %all-to-all-done.1 = f32[8,1,64]{2,1,0:T(1,128)S(1)} async-done(((f32[8,1,64]{2,1,0:T(1,128)}), f32[8,1,64]{2,1,0:T(1,128)S(1)}, u32[]{:S(2)}, u32[]{:S(2)}) %all-to-all-start.1) | async-done | bytes 2080 | tf_op jit(solution)/shard_map/all_to_all | solution.py:75
  174.7 3.3 %all-to-all-start.4 = ((f32[8,1,64]{2,1,0:T(1,128)}), f32[8,1,64]{2,1,0:T(1,128)S(1)}, u32[]{:S(2)}, u32[]{:S(2)}) async-start(f32[8,1,64]{2,1,0:T(1,128)} %all_to_all.43), calls=%async_computation.4 | async-start | bytes 8192 | tf_op jit(solution)/shard_map/all_to_all | solution.py:77
  178.0 0.5 broadcast.181
  178.5 0.7 reduce.27
  179.2 0.1 reshape.381
  179.3 1.9 gather_fusion.1
  181.2 0.1 reshape.382
  181.3 0.7 reduce.26
  182.0 0.1 reshape.379
  182.1 1.9 gather_fusion
  184.0 0.1 reshape.380
  184.2 0.1 reduce_max.19
  184.3 0.7 reduce.29
  185.0 0.1 reshape.384
  185.1 1.9 gather_fusion.2
  187.0 0.1 reshape.385
  187.1 0.1 reduce_sum.80
  187.3 0.2 multiply_reduce_fusion
  187.4 0.5 fusion.21
  188.0 0.1 broadcast_in_dim.55
  188.1 0.1 reshape.441
  188.2 1.4 scatter_custom_fusion.2
  189.6 0.1 all_to_all.45
  189.7 12.2 %all_to_all.57 = f32[8,1,64]{2,1,0:T(1,128)S(1)} all-to-all(f32[8,1,64]{2,1,0:T(1,128)S(1)} %all_to_all.45), channel_id=1, replica_groups=mesh['own'=8,'rep'=4] {'own'}, dimensions={0} | all-to-all | bytes 4096 | tf_op jit(solution)/shard_map/all_to_all | solution.py:87
  201.9 0.7 reduce.30
  202.5 0.1 sub.109
  202.6 3.3 %subtract_convert_fusion = bf16[512,2048]{1,0:T(8,128)(2,1)S(1)} fusion(f32[512,2048]{1,0:T(8,128)} %reduce.7, f32[512]{0:T(512)S(1)} %sub.109, s32[512]{0:T(512)S(1)} %eq.98), kind=kLoop, calls=%fused_computation.12 | loop fusion | flops 5242880 | bytes 6295552 | tf_op jit(solution)/shard_map/convert_element_type | solution.py:100
  205.9 1.5 fusion.8
  207.4 3.5 %all-to-all-start.6 = ((f32[8,64,256]{2,1,0:T(8,128)}), f32[8,64,256]{2,1,0:T(8,128)S(1)}, u32[]{:S(2)}, u32[]{:S(2)}) async-start(f32[8,64,256]{2,1,0:T(8,128)} %fusion.8), calls=%async_computation.6 | async-start | bytes 1048576 | tf_op jit(solution)/shard_map/all_to_all | solution.py:109
  210.9 4.7 %fusion.3 = bf16[1,2048,256]{2,1,0:T(8,128)(2,1)} fusion(bf16[512,256]{1,0:T(8,128)(2,1)S(1)} %bitcast.46, f32[512,2048]{1,0:T(8,128)} %reduce.7, s32[512]{0:T(512)S(1)} %eq.98, f32[512]{0:T(512)S(1)} %sub.109), kind=kOutput, calls=%fused_computation.17 | convolution fusion | flops 542638080 | bytes 5509120 | tf_op jit(solution)/shard_map/brc,brd->bcd/dot_general | solution.py:101
  215.7 6.1 %all-to-all-done.6 = f32[8,64,256]{2,1,0:T(8,128)S(1)} async-done(((f32[8,64,256]{2,1,0:T(8,128)}), f32[8,64,256]{2,1,0:T(8,128)S(1)}, u32[]{:S(2)}, u32[]{:S(2)}) %all-to-all-start.6) | async-done | bytes 524320 | tf_op jit(solution)/shard_map/all_to_all | solution.py:109
  221.8 1.0 gather_fusion.3
  222.7 0.1 reshape.388
  222.9 1.0 reduce_sum.81
  (13 shorter events, 0.1 us)
Async XLA Ops:
  7.2 21.3 %copy-start = (bf16[1,2048,256]{2,1,0:T(8,128)(2,1)S(1)}, bf16[1,2048,256]{2,1,0:T(8,128)(2,1)}, u32[]{:S(2)}) copy-start(bf16[1,2048,256]{2,1,0:T(8,128)(2,1)} %param.6) | copy-start | bytes 3145732
  7.2 129.1 %all-gather.3.cloned.1.call-start = ((), (), s32[]{:S(2)}) async-start(), calls=%async_computation.7 | async-start | bytes 20971520 | tf_op jit(solution)/shard_map/all_gather | solution.py:61
  28.5 2.7 %copy-start.1 = (s32[128]{0:T(128)S(1)}, s32[128]{0:T(128)}, u32[]{:S(2)}) copy-start(s32[128]{0:T(128)} %param.9) | copy-start | bytes 1540
  153.1 11.9 %all-to-all-start.2 = ((f32[8,1,64]{2,1,0:T(1,128)}), f32[8,1,64]{2,1,0:T(1,128)S(1)}, u32[]{:S(2)}, u32[]{:S(2)}) async-start(f32[8,1,64]{2,1,0:T(1,128)} %all_to_all.39), calls=%async_computation.2 | async-start | bytes 8192 | tf_op jit(solution)/shard_map/all_to_all | solution.py:76
  165.0 9.6 %all-to-all-start.1 = ((f32[8,1,64]{2,1,0:T(1,128)}), f32[8,1,64]{2,1,0:T(1,128)S(1)}, u32[]{:S(2)}, u32[]{:S(2)}) async-start(f32[8,1,64]{2,1,0:T(1,128)} %all_to_all.37), calls=%async_computation.1 | async-start | bytes 8192 | tf_op jit(solution)/shard_map/all_to_all | solution.py:75
  174.7 9.6 %all-to-all-start.4 = ((f32[8,1,64]{2,1,0:T(1,128)}), f32[8,1,64]{2,1,0:T(1,128)S(1)}, u32[]{:S(2)}, u32[]{:S(2)}) async-start(f32[8,1,64]{2,1,0:T(1,128)} %all_to_all.43), calls=%async_computation.4 | async-start | bytes 8192 | tf_op jit(solution)/shard_map/all_to_all | solution.py:77
  207.4 14.3 %all-to-all-start.6 = ((f32[8,64,256]{2,1,0:T(8,128)}), f32[8,64,256]{2,1,0:T(8,128)S(1)}, u32[]{:S(2)}, u32[]{:S(2)}) async-start(f32[8,64,256]{2,1,0:T(8,128)} %fusion.8), calls=%async_computation.6 | async-start | bytes 1048576 | tf_op jit(solution)/shard_map/all_to_all | solution.py:109
Sparse Core Ops, SparseCore 0:
  31.3 104.9 all-gather.2
